TPU v7x, 32 devices: a whole 2x2x4 slice. The times are simulated.
32 devices in a mesh: dp: 16 (over z, y, x), tensor: 2 (over core).
Axes of the slice: x: 2, y: 2, z: 4, core: 2. Of those that a mesh axis runs over, the one named last changes fastest.
Arguments:
- acts: bfloat16 [1, 6144, 28672], P(None, 'dp', 'tensor'), may hold values from -6 to 6
- out_grads: bfloat16 [1, 6144, 8192], P(None, 'dp', 'tensor'), may hold values from -6 to 6
- proj_in: bfloat16 [1, 28672, 64], P(None, 'tensor'), may hold values from -0.03125 to 0.03125
- proj_out: bfloat16 [1, 8192, 64], P(None, 'tensor'), may hold values from -0.0625 to 0.0625
- doc_starts: int32 [64], P('dp'), may hold values from 0 to 191, as said below
- token_counts: int32 [16], P('dp'), may hold values from 192 to 384, as said below
- queries: float32 [256, 1, 4096], P('dp', None, 'tensor'), may hold values from -0.046875 to 0.046875
Outputs:
- scores: float32 [256, 64], P(None, 'dp')
- doc_grads: float32 [64, 1, 4096], P('dp', None, 'tensor')
Inputs may be any that keep to these rules, and one draw needn't show every extreme that they name: `doc_starts`: within each block of 4 entries the first is 0, the entries rise strictly, and the last is 191. `token_counts`: entry 0 equals 384.
All inputs are finite; a program needn't handle non-finite values.
Results may differ from a plain program's by a relative error of at most 0.0003.
Values sent between devices are 32-bit elements; how exact they have to be, the bound alone decides.
A program may use at most 64 MiB of HBM per device.

v0:
```python
import jax
import jax.numpy as jnp
from jax import lax
from jax.sharding import PartitionSpec as P


def document_products(member, left, right):
    spread = member[None, :, :, None] * left[:, :, None, :]
    grads = jnp.einsum("ltdr,lts->dlrs", spread, right, precision=lax.Precision.HIGHEST)
    return grads.reshape(grads.shape[0], grads.shape[1], grads.shape[2] * grads.shape[3])


def shards(acts, out_grads, proj_in, proj_out, doc_starts, token_counts, queries):
    layer_count = acts.shape[0]
    tok_rows = acts.shape[1]
    rank_size = proj_in.shape[2]
    docs_local = doc_starts.shape[0]
    left = jnp.stack([jnp.dot(acts[0], proj_in[0], preferred_element_type=jnp.float32)])
    right = jnp.stack([jnp.dot(out_grads[0], proj_out[0], preferred_element_type=jnp.float32)])
    positions = jnp.arange(tok_rows, dtype=jnp.int32)
    doc_index = jnp.sum((positions[:, None] >= doc_starts[None, :]).astype(jnp.int32), axis=1) - 1
    valid = positions < token_counts[0]
    member = (
        (doc_index[:, None] == jnp.arange(docs_local, dtype=jnp.int32)[None, :]) & valid[:, None]
    ).astype(jnp.float32)
    width = lax.axis_size("tensor")
    slot = lax.axis_index("tensor")
    share_width = rank_size * rank_size // width
    left, right = lax.psum((left, right), "tensor")
    full_grads = document_products(member, left, right)
    mine = lax.dynamic_slice_in_dim(full_grads, slot * share_width, share_width, 2)
    flat_grads = mine.reshape(docs_local, layer_count * share_width)
    piece = lax.all_gather(queries, "dp", axis=0, tiled=True)
    rows = piece.reshape(piece.shape[0], layer_count * share_width)
    partial_scores = jnp.dot(
        rows, flat_grads.T, precision=lax.Precision.HIGHEST, preferred_element_type=jnp.float32
    )
    scores = lax.psum(partial_scores, "tensor")
    return (scores, mine)


def solution(mesh):
    in_specs = (
        P(None, "dp", "tensor"),
        P(None, "dp", "tensor"),
        P(None, "tensor", None),
        P(None, "tensor", None),
        P("dp"),
        P("dp"),
        P("dp", None, "tensor"),
    )
    out_specs = (P(None, "dp"), P("dp", None, "tensor"))
    return jax.shard_map(shards, mesh=mesh, in_specs=in_specs, out_specs=out_specs, check_vma=False)
```

profile of v0, /device:TPU:0, one launch (start us, length us, event | category | flops | bytes accessed | tf_op | source)
XLA Modules:
  0.0 99.2 jit_solution(14235674293041148226)
XLA Ops:
  8.0 0.0 copy-start
  8.0 0.0 all-reduce.3.cloned.1.call-start
  8.1 0.0 copy-start.1
  8.1 8.9 %fusion = f32[384,64]{0,1:T(8,128)} fusion(bf16[1,384,14336]{2,1,0:T(8,128)(2,1)} %param.7, bf16[1,14336,64]{1,2,0:T(8,128)(2,1)} %param.9), kind=kOutput, calls=%fused_computation | convolution fusion | flops 704643072 | bytes 12943360 | tf_op jit(solution)/shard_map/dot_general | solution.py:18
  17.0 0.0 copy-done
  17.0 0.0 copy-done.1
  17.0 0.0 copy-start.2
  17.0 1.7 %fusion.2 = f32[384,64]{0,1:T(8,128)} fusion(bf16[1,384,4096]{2,1,0:T(8,128)(2,1)S(1)} %copy-done, bf16[1,4096,64]{1,2,0:T(8,128)(2,1)S(1)} %copy-done.1), kind=kOutput, calls=%fused_computation.2 | convolution fusion | flops 201326592 | bytes 3768320 | tf_op jit(solution)/shard_map/dot_general | solution.py:19
  18.7 0.0 all-reduce.3.cloned.1.call-update
  18.7 0.0 all-gather.2.cloned.1.call-start
  18.8 0.5 all-gather.2.cloned.1.call-update
  20.0 0.0 copy-done.2
  20.0 0.1 convert_reduce_fusion
  20.1 19.6 %all-reduce.3.cloned.1.call-done = (f32[384,64]{0,1:T(8,128)}, f32[384,64]{0,1:T(8,128)}) async-done(((f32[384,64]{0,1:T(8,128)}, f32[384,64]{0,1:T(8,128)}), (f32[384,64]{0,1:T(8,128)}, f32[384,64]{0,1:T(8,128)})) %all-reduce.3.cloned.1.call-update) | async-done | bytes 196624 | tf_op jit(solution)/shard_map/psum | solution.py:29
  39.7 1.8 %convolution_bitcast_fusion = f32[4,1,64,64]{2,3,0,1:T(8,128)S(1)} fusion(f32[384,64]{0,1:T(8,128)} %get-tuple-element.8, f32[384,4]{0,1:T(4,128)S(1)} %fusion.18, f32[384,64]{0,1:T(8,128)} %get-tuple-element.9), kind=kOutput, calls=%fused_computation.8 | convolution fusion | flops 75595776 | bytes 268288 | tf_op jit(solution)/shard_map/ltdr,lts->dlrs/dot_general | solution.py:9
  41.5 0.1 copy.13
  41.6 0.1 reshape.72
  41.8 0.6 copy.14
  42.4 42.8 %all-gather.2.cloned.1.call-done = f32[256,1,2048]{2,1,0:T(1,128)} async-done(((f32[16,1,2048]{2,1,0:T(1,128)}), f32[256,1,2048]{2,1,0:T(1,128)}) %all-gather.2.cloned.1.call-update) | async-done | bytes 2097168 | tf_op jit(solution)/shard_map/all_gather | solution.py:33
  85.2 3.5 %fusion.8 = f32[256,4]{0,1:T(4,128)S(1)} fusion(f32[256,1,2048]{2,1,0:T(1,128)} %all-gather.2.cloned.1.call-done, f32[4,1,2048]{2,0,1:T(4,128)S(1)} %constant_dynamic-slice_fusion), kind=kOutput, calls=%fused_computation.9 | convolution fusion | flops 25165824 | bytes 2134016 | tf_op jit(solution)/shard_map/dot_general | solution.py:35
  88.7 3.1 %psum.23 = f32[256,4]{0,1:T(4,128)} all-reduce(f32[256,4]{0,1:T(4,128)S(1)} %fusion.8), channel_id=1, replica_groups=mesh['dp'=16,'tensor'=2] {'tensor'}, use_global_device_ids=true, to_apply=%region_3.0 | all-reduce | flops 1024 | bytes 8192 | tf_op jit(solution)/shard_map/psum | solution.py:38
  (4 shorter events, 0.0 us)
Async XLA Ops:
  8.0 9.0 %copy-start = (bf16[1,384,4096]{2,1,0:T(8,128)(2,1)S(1)}, bf16[1,384,4096]{2,1,0:T(8,128)(2,1)}, u32[]{:S(2)}) copy-start(bf16[1,384,4096]{2,1,0:T(8,128)(2,1)} %param.8) | copy-start | bytes 9437188
  8.0 31.7 %all-reduce.3.cloned.1.call-start = ((), (), s32[]{:S(2)}) async-start(), calls=%async_computation.1 | async-start | bytes 393216 | tf_op jit(solution)/shard_map/psum | solution.py:29
  8.1 8.9 %copy-start.1 = (bf16[1,4096,64]{1,2,0:T(8,128)(2,1)S(1)}, bf16[1,4096,64]{1,2,0:T(8,128)(2,1)}, u32[]{:S(2)}) copy-start(bf16[1,4096,64]{1,2,0:T(8,128)(2,1)} %param.10) | copy-start | bytes 1572868
  17.0 3.0 %copy-start.2 = (s32[4]{0:T(128)S(1)}, s32[4]{0:T(128)}, u32[]{:S(2)}) copy-start(s32[4]{0:T(128)} %param.11) | copy-start | bytes 52
  18.7 66.5 %all-gather.2.cloned.1.call-start = ((), (), s32[]{:S(2)}) async-start(), calls=%async_computation | async-start | bytes 2228224 | tf_op jit(solution)/shard_map/all_gather | solution.py:33
Sparse Core Ops, SparseCore 0:
  18.8 20.8 all-reduce.2
Sparse Core Ops, SparseCore 1:
  22.0 63.2 all-gather.1
where the time goes:
time: 99.4 us; the launch traced here: 99.2 us
  waiting for transfers between devices  63 us (63%)
  between operations  16.2 us (16%)
  matrix products  15.9 us (16%)
  blocking collectives  3.05 us (3%)
    all_gather x1, waiting for transfers between devices, shards(): piece = lax.all_gather(queries, 'dp', axis=0, tiled=True)  42.8 us
    psum x1, waiting for transfers between devices, shards(): left, right = lax.psum((left, right), 'tensor')  19.6 us
    dot_general x1, matrix products, shards(): jnp.dot(acts[0], proj_in[0], preferred_element_type=jnp.float32)  8.88 us
    dot_general x1, matrix products, shards(): jnp.dot(rows, flat_grads.T, precision=lax.Precision.HIGHEST, preferred_el...  3.52 us
    psum x1, blocking collectives, shards(): scores = lax.psum(partial_scores, 'tensor')  3.05 us
  transfers between devices with their start and end apart: 2, of which 2 were waited for; matrix products, arithmetic and copies ran while one was open for 3% of the time, Pallas kernels for 0%

commit v1 on v0

--- a/solution.py
+++ b/solution.py
@@ -30,7 +30,12 @@
     full_grads = document_products(member, left, right)
     mine = lax.dynamic_slice_in_dim(full_grads, slot * share_width, share_width, 2)
     flat_grads = mine.reshape(docs_local, layer_count * share_width)
-    piece = lax.all_gather(queries, "dp", axis=0, tiled=True)
+    ring = [queries]
+    for hop in range(15):
+        ring.append(lax.ppermute(ring[-1], "dp", [(dev, (dev + 1) % 16) for dev in range(16)]))
+    piece = jnp.roll(
+        jnp.concatenate(ring[::-1], axis=0), (lax.axis_index("dp") + 1) * ring[0].shape[0], axis=0
+    )
     rows = piece.reshape(piece.shape[0], layer_count * share_width)
     partial_scores = jnp.dot(
         rows, flat_grads.T, precision=lax.Precision.HIGHEST, preferred_element_type=jnp.float32

time: 99.4 us -> 176 us (1.77)
  waiting for transfers between devices: 63 us -> 112 us
  local copies, waits for them, and re-layouts: 0.88 us -> 25.2 us
  starting transfers between devices: 0.08 us -> 4.97 us
    ppermute x0 -> x15, waiting for transfers between devices: none -> 108 us  [shards(): lax.ppermute(ring[-1], 'dp', [(dev, (dev + 1) % 16) for dev in range(16)])]
    all_gather x1 -> x0, waiting for transfers between devices: 42.8 us -> none  [shards(): piece = lax.all_gather(queries, 'dp', axis=0, tiled=True)]
    unnamed x7 -> x72, local copies, waits for them, and re-layouts: 0.67 us -> 19.7 us
    psum x1, waiting for transfers between devices: 19.6 us -> 4.16 us  [shards(): left, right = lax.psum((left, right), 'tensor')]
    ppermute x0 -> x15, starting transfers between devices: none -> 4.94 us  [shards(): lax.ppermute(ring[-1], 'dp', [(dev, (dev + 1) % 16) for dev in range(16)])]
  transfers between devices with their start and end apart: 2 -> 16, of which waited for: 2 -> 14; matrix products, arithmetic and copies ran while one was open for 3% -> 10% of each run, Pallas kernels for 0% -> 0%
where the time goes in v1:
time: 176 us
  waiting for transfers between devices  112 us (64%)
  local copies, waits for them, and re-layouts  25.2 us (14%)
  matrix products  15.1 us (9%)
  between operations  15.1 us (9%)
  starting transfers between devices  4.97 us (3%)
  blocking collectives  3.05 us (2%)
    ppermute x15, waiting for transfers between devices, shards(): lax.ppermute(ring[-1], 'dp', [(dev, (dev + 1) % 16) for dev in range(16)])  108 us
    unnamed x72, local copies, waits for them, and re-layouts  19.7 us
    dot_general x1, matrix products, shards(): jnp.dot(acts[0], proj_in[0], preferred_element_type=jnp.float32)  8.78 us
    ppermute x15, starting transfers between devices, shards(): lax.ppermute(ring[-1], 'dp', [(dev, (dev + 1) % 16) for dev in range(16)])  4.94 us
    psum x1, waiting for transfers between devices, shards(): left, right = lax.psum((left, right), 'tensor')  4.16 us
  transfers between devices with their start and end apart: 16, of which 14 were waited for; matrix products, arithmetic and copies ran while one was open for 10% of the time, Pallas kernels for 0%

profile of v1, /device:TPU:0, one launch (start us, length us, event | category | flops | bytes accessed | tf_op | source)
XLA Modules:
  0.0 175.6 jit_solution(6254717181464085074)
XLA Ops:
  7.2 3.0 %collective-permute-start = (f32[16,1,2048]{2,1,0:T(1,128)}, f32[16,1,2048]{2,1,0:T(1,128)S(1)}, u32[]{:S(2)}, u32[]{:S(2)}) collective-permute-start(f32[16,1,2048]{2,1,0:T(1,128)} %param.13), channel_id=1, source_target_pairs={{0,2},{2,4},{4,6},{6,8},{8,10},{10,12},{12,14},{14,16},{16,18},{18... | collective-permute-start | bytes 393224 | tf_op jit(solution)/shard_map/ppermute | solution.py:35
  10.3 7.7 %collective-permute-done = f32[16,1,2048]{2,1,0:T(1,128)S(1)} collective-permute-done((f32[16,1,2048]{2,1,0:T(1,128)}, f32[16,1,2048]{2,1,0:T(1,128)S(1)}, u32[]{:S(2)}, u32[]{:S(2)}) %collective-permute-start) | collective-permute-done | bytes 131104 | tf_op jit(solution)/shard_map/ppermute | solution.py:35
  18.0 8.6 %collective-permute-done.1 = f32[16,1,2048]{2,1,0:T(1,128)S(1)} collective-permute-done((f32[16,1,2048]{2,1,0:T(1,128)S(1)}, f32[16,1,2048]{2,1,0:T(1,128)S(1)}, u32[]{:S(2)}, u32[]{:S(2)}) %collective-permute-start.1) | collective-permute-done | bytes 131104 | tf_op jit(solution)/shard_map/ppermute | solution.py:35
  26.5 8.6 %collective-permute-done.2 = f32[16,1,2048]{2,1,0:T(1,128)S(1)} collective-permute-done((f32[16,1,2048]{2,1,0:T(1,128)S(1)}, f32[16,1,2048]{2,1,0:T(1,128)S(1)}, u32[]{:S(2)}, u32[]{:S(2)}) %collective-permute-start.2) | collective-permute-done | bytes 131104 | tf_op jit(solution)/shard_map/ppermute | solution.py:35
  35.1 8.6 %collective-permute-done.3 = f32[16,1,2048]{2,1,0:T(1,128)S(1)} collective-permute-done((f32[16,1,2048]{2,1,0:T(1,128)S(1)}, f32[16,1,2048]{2,1,0:T(1,128)S(1)}, u32[]{:S(2)}, u32[]{:S(2)}) %collective-permute-start.3) | collective-permute-done | bytes 131104 | tf_op jit(solution)/shard_map/ppermute | solution.py:35
  44.3 8.6 %collective-permute-done.4 = f32[16,1,2048]{2,1,0:T(1,128)S(1)} collective-permute-done((f32[16,1,2048]{2,1,0:T(1,128)S(1)}, f32[16,1,2048]{2,1,0:T(1,128)S(1)}, u32[]{:S(2)}, u32[]{:S(2)}) %collective-permute-start.4) | collective-permute-done | bytes 131104 | tf_op jit(solution)/shard_map/ppermute | solution.py:35
  53.5 8.6 %collective-permute-done.5 = f32[16,1,2048]{2,1,0:T(1,128)S(1)} collective-permute-done((f32[16,1,2048]{2,1,0:T(1,128)S(1)}, f32[16,1,2048]{2,1,0:T(1,128)S(1)}, u32[]{:S(2)}, u32[]{:S(2)}) %collective-permute-start.5) | collective-permute-done | bytes 131104 | tf_op jit(solution)/shard_map/ppermute | solution.py:35
  62.7 9.4 %collective-permute-done.6 = f32[16,1,2048]{2,1,0:T(1,128)S(1)} collective-permute-done((f32[16,1,2048]{2,1,0:T(1,128)S(1)}, f32[16,1,2048]{2,1,0:T(1,128)S(1)}, u32[]{:S(2)}, u32[]{:S(2)}) %collective-permute-start.6) | collective-permute-done | bytes 131104 | tf_op jit(solution)/shard_map/ppermute | solution.py:35
  72.7 9.4 %collective-permute-done.7 = f32[16,1,2048]{2,1,0:T(1,128)S(1)} collective-permute-done((f32[16,1,2048]{2,1,0:T(1,128)S(1)}, f32[16,1,2048]{2,1,0:T(1,128)S(1)}, u32[]{:S(2)}, u32[]{:S(2)}) %collective-permute-start.7) | collective-permute-done | bytes 131104 | tf_op jit(solution)/shard_map/ppermute | solution.py:35
  82.8 8.6 %collective-permute-done.8 = f32[16,1,2048]{2,1,0:T(1,128)S(1)} collective-permute-done((f32[16,1,2048]{2,1,0:T(1,128)S(1)}, f32[16,1,2048]{2,1,0:T(1,128)S(1)}, u32[]{:S(2)}, u32[]{:S(2)}) %collective-permute-start.8) | collective-permute-done | bytes 131104 | tf_op jit(solution)/shard_map/ppermute | solution.py:35
  92.0 8.6 %collective-permute-done.9 = f32[16,1,2048]{2,1,0:T(1,128)S(1)} collective-permute-done((f32[16,1,2048]{2,1,0:T(1,128)S(1)}, f32[16,1,2048]{2,1,0:T(1,128)S(1)}, u32[]{:S(2)}, u32[]{:S(2)}) %collective-permute-start.9) | collective-permute-done | bytes 131104 | tf_op jit(solution)/shard_map/ppermute | solution.py:35
  100.6 8.8 %fusion = f32[384,64]{0,1:T(8,128)} fusion(bf16[1,384,14336]{2,1,0:T(8,128)(2,1)} %param.7, bf16[1,14336,64]{1,2,0:T(8,128)(2,1)} %param.9), kind=kOutput, calls=%fused_computation | convolution fusion | flops 704643072 | bytes 12943360 | tf_op jit(solution)/shard_map/dot_general | solution.py:18
  109.5 1.7 fusion.2
  111.3 7.0 %collective-permute-done.11 = f32[16,1,2048]{2,1,0:T(1,128)} collective-permute-done((f32[16,1,2048]{2,1,0:T(1,128)}, f32[16,1,2048]{2,1,0:T(1,128)}, u32[]{:S(2)}, u32[]{:S(2)}) %collective-permute-start.11) | collective-permute-done | bytes 131104 | tf_op jit(solution)/shard_map/ppermute | solution.py:35
  119.0 8.2 %collective-permute-done.12 = f32[16,1,2048]{2,1,0:T(1,128)} collective-permute-done((f32[16,1,2048]{2,1,0:T(1,128)}, f32[16,1,2048]{2,1,0:T(1,128)}, u32[]{:S(2)}, u32[]{:S(2)}) %collective-permute-start.12) | collective-permute-done | bytes 131104 | tf_op jit(solution)/shard_map/ppermute | solution.py:35
  127.3 4.2 %all-reduce.3.cloned.1.call-done = (f32[384,64]{0,1:T(8,128)}, f32[384,64]{0,1:T(8,128)}) async-done(((f32[384,64]{0,1:T(8,128)}, f32[384,64]{0,1:T(8,128)}), (f32[384,64]{0,1:T(8,128)}, f32[384,64]{0,1:T(8,128)})) %all-reduce.3.cloned.1.call-update) | async-done | bytes 196624 | tf_op jit(solution)/shard_map/psum | solution.py:29
  131.4 2.5 %convolution_bitcast_fusion = f32[4,1,64,64]{2,3,0,1:T(8,128)} fusion(f32[384,64]{0,1:T(8,128)} %get-tuple-element.6, f32[384,4]{0,1:T(4,128)S(1)} %fusion.15, f32[384,64]{0,1:T(8,128)} %get-tuple-element.7), kind=kOutput, calls=%fused_computation.8 | convolution fusion | flops 75595776 | bytes 268288 | tf_op jit(solution)/shard_map/ltdr,lts->dlrs/dot_general | solution.py:9
  133.9 1.7 copy.11
  135.5 1.6 reshape.73
  137.2 1.8 %collective-permute-start.14 = (f32[16,1,2048]{2,1,0:T(1,128)}, f32[16,1,2048]{2,1,0:T(1,128)S(1)}, u32[]{:S(2)}, u32[]{:S(2)}) collective-permute-start(f32[16,1,2048]{2,1,0:T(1,128)} %collective-permute-done.13), channel_id=1, source_target_pairs={{0,2},{2,4},{4,6},{6,8},{8,10},{10,12},{12,14},{14,16},{16,18},{18... | collective-permute-start | bytes 393224 | tf_op jit(solution)/shard_map/ppermute | solution.py:35
  140.5 6.4 %collective-permute-done.14 = f32[16,1,2048]{2,1,0:T(1,128)S(1)} collective-permute-done((f32[16,1,2048]{2,1,0:T(1,128)}, f32[16,1,2048]{2,1,0:T(1,128)S(1)}, u32[]{:S(2)}, u32[]{:S(2)}) %collective-permute-start.14) | collective-permute-done | bytes 131104 | tf_op jit(solution)/shard_map/ppermute | solution.py:35
  146.9 0.9 constant_dynamic-update-slice_fusion.30
  147.8 0.9 constant_dynamic-update-slice_fusion.29
  148.7 0.9 constant_dynamic-update-slice_fusion.28
  149.6 0.9 constant_dynamic-update-slice_fusion.27
  150.6 0.9 constant_dynamic-update-slice_fusion.26
  151.5 0.9 constant_dynamic-update-slice_fusion.25
  153.4 0.9 constant_dynamic-update-slice_fusion.23
  154.3 0.9 constant_dynamic-update-slice_fusion.22
  162.2 1.4 constant_dynamic-slice_fusion.1
  163.7 2.1 %fusion.4 = f32[256,4]{0,1:T(4,128)S(1)} fusion(f32[256,1,2048]{2,1,0:T(1,128)S(1)} %constant_dynamic-slice_fusion.1, f32[4,1,2048]{2,0,1:T(4,128)S(1)} %constant_dynamic-slice_fusion), kind=kOutput, calls=%fused_computation.4 | convolution fusion | flops 25165824 | bytes 2134016 | tf_op jit(solution)/shard_map/dot_general | solution.py:40
  165.7 3.0 %psum.23 = f32[256,4]{0,1:T(4,128)} all-reduce(f32[256,4]{0,1:T(4,128)S(1)} %fusion.4), channel_id=1, replica_groups=mesh['dp'=16,'tensor'=2] {'tensor'}, use_global_device_ids=true, to_apply=%region_3.4 | all-reduce | flops 1024 | bytes 8192 | tf_op jit(solution)/shard_map/psum | solution.py:43
  (87 shorter events, 13.3 us)
Async XLA Ops:
  7.2 102.3 %copy-start = (bf16[1,384,4096]{2,1,0:T(8,128)(2,1)S(1)}, bf16[1,384,4096]{2,1,0:T(8,128)(2,1)}, u32[]{:S(2)}) copy-start(bf16[1,384,4096]{2,1,0:T(8,128)(2,1)} %param.8) | copy-start | bytes 9437188
  7.2 124.2 %all-reduce.3.cloned.1.call-start = ((), (), s32[]{:S(2)}) async-start(), calls=%async_computation | async-start | bytes 393216 | tf_op jit(solution)/shard_map/psum | solution.py:29
  7.2 102.3 %copy-start.1 = (bf16[1,4096,64]{1,2,0:T(8,128)(2,1)S(1)}, bf16[1,4096,64]{1,2,0:T(8,128)(2,1)}, u32[]{:S(2)}) copy-start(bf16[1,4096,64]{1,2,0:T(8,128)(2,1)} %param.10) | copy-start | bytes 1572868
  7.2 10.7 %collective-permute-start = (f32[16,1,2048]{2,1,0:T(1,128)}, f32[16,1,2048]{2,1,0:T(1,128)S(1)}, u32[]{:S(2)}, u32[]{:S(2)}) collective-permute-start(f32[16,1,2048]{2,1,0:T(1,128)} %param.13), channel_id=1, source_target_pairs={{0,2},{2,4},{4,6},{6,8},{8,10},{10,12},{12,14},{14,16},{16,18},{18... | collective-permute-start | bytes 393224 | tf_op jit(solution)/shard_map/ppermute | solution.py:35
  18.0 8.6 %collective-permute-start.1 = (f32[16,1,2048]{2,1,0:T(1,128)S(1)}, f32[16,1,2048]{2,1,0:T(1,128)S(1)}, u32[]{:S(2)}, u32[]{:S(2)}) collective-permute-start(f32[16,1,2048]{2,1,0:T(1,128)S(1)} %collective-permute-done), channel_id=1, source_target_pairs={{0,2},{2,4},{4,6},{6,8},{8,10},{10,12},{12,14},{14,16},{16,18},{18... | collective-permute-start | bytes 393224 | tf_op jit(solution)/shard_map/ppermute | solution.py:35
  26.5 8.6 %collective-permute-start.2 = (f32[16,1,2048]{2,1,0:T(1,128)S(1)}, f32[16,1,2048]{2,1,0:T(1,128)S(1)}, u32[]{:S(2)}, u32[]{:S(2)}) collective-permute-start(f32[16,1,2048]{2,1,0:T(1,128)S(1)} %collective-permute-done.1), channel_id=1, source_target_pairs={{0,2},{2,4},{4,6},{6,8},{8,10},{10,12},{12,14},{14,16},{16,18},{18... | collective-permute-start | bytes 393224 | tf_op jit(solution)/shard_map/ppermute | solution.py:35
  35.1 65.5 %copy-start.3 = (f32[16,1,2048]{2,1,0:T(1,128)}, f32[16,1,2048]{2,1,0:T(1,128)S(1)}, u32[]{:S(2)}) copy-start(f32[16,1,2048]{2,1,0:T(1,128)S(1)} %collective-permute-done.2) | copy-start | bytes 393220
  35.1 8.6 %collective-permute-start.3 = (f32[16,1,2048]{2,1,0:T(1,128)S(1)}, f32[16,1,2048]{2,1,0:T(1,128)S(1)}, u32[]{:S(2)}, u32[]{:S(2)}) collective-permute-start(f32[16,1,2048]{2,1,0:T(1,128)S(1)} %collective-permute-done.2), channel_id=1, source_target_pairs={{0,2},{2,4},{4,6},{6,8},{8,10},{10,12},{12,14},{14,16},{16,18},{18... | collective-permute-start | bytes 393224 | tf_op jit(solution)/shard_map/ppermute | solution.py:35
  44.3 8.6 %collective-permute-start.4 = (f32[16,1,2048]{2,1,0:T(1,128)S(1)}, f32[16,1,2048]{2,1,0:T(1,128)S(1)}, u32[]{:S(2)}, u32[]{:S(2)}) collective-permute-start(f32[16,1,2048]{2,1,0:T(1,128)S(1)} %collective-permute-done.3), channel_id=1, source_target_pairs={{0,2},{2,4},{4,6},{6,8},{8,10},{10,12},{12,14},{14,16},{16,18},{18... | collective-permute-start | bytes 393224 | tf_op jit(solution)/shard_map/ppermute | solution.py:35
  53.5 8.6 %collective-permute-start.5 = (f32[16,1,2048]{2,1,0:T(1,128)S(1)}, f32[16,1,2048]{2,1,0:T(1,128)S(1)}, u32[]{:S(2)}, u32[]{:S(2)}) collective-permute-start(f32[16,1,2048]{2,1,0:T(1,128)S(1)} %collective-permute-done.4), channel_id=1, source_target_pairs={{0,2},{2,4},{4,6},{6,8},{8,10},{10,12},{12,14},{14,16},{16,18},{18... | collective-permute-start | bytes 393224 | tf_op jit(solution)/shard_map/ppermute | solution.py:35
  62.1 0.7 copy-start.9
  62.7 9.4 %collective-permute-start.6 = (f32[16,1,2048]{2,1,0:T(1,128)S(1)}, f32[16,1,2048]{2,1,0:T(1,128)S(1)}, u32[]{:S(2)}, u32[]{:S(2)}) collective-permute-start(f32[16,1,2048]{2,1,0:T(1,128)S(1)} %collective-permute-done.5), channel_id=1, source_target_pairs={{0,2},{2,4},{4,6},{6,8},{8,10},{10,12},{12,14},{14,16},{16,18},{18... | collective-permute-start | bytes 393224 | tf_op jit(solution)/shard_map/ppermute | solution.py:35
  72.7 9.4 %collective-permute-start.7 = (f32[16,1,2048]{2,1,0:T(1,128)S(1)}, f32[16,1,2048]{2,1,0:T(1,128)S(1)}, u32[]{:S(2)}, u32[]{:S(2)}) collective-permute-start(f32[16,1,2048]{2,1,0:T(1,128)S(1)} %collective-permute-done.6), channel_id=1, source_target_pairs={{0,2},{2,4},{4,6},{6,8},{8,10},{10,12},{12,14},{14,16},{16,18},{18... | collective-permute-start | bytes 393224 | tf_op jit(solution)/shard_map/ppermute | solution.py:35
  82.2 0.7 copy-start.13
  82.8 8.6 %collective-permute-start.8 = (f32[16,1,2048]{2,1,0:T(1,128)S(1)}, f32[16,1,2048]{2,1,0:T(1,128)S(1)}, u32[]{:S(2)}, u32[]{:S(2)}) collective-permute-start(f32[16,1,2048]{2,1,0:T(1,128)S(1)} %collective-permute-done.7), channel_id=1, source_target_pairs={{0,2},{2,4},{4,6},{6,8},{8,10},{10,12},{12,14},{14,16},{16,18},{18... | collective-permute-start | bytes 393224 | tf_op jit(solution)/shard_map/ppermute | solution.py:35
  92.0 8.6 %collective-permute-start.9 = (f32[16,1,2048]{2,1,0:T(1,128)S(1)}, f32[16,1,2048]{2,1,0:T(1,128)S(1)}, u32[]{:S(2)}, u32[]{:S(2)}) collective-permute-start(f32[16,1,2048]{2,1,0:T(1,128)S(1)} %collective-permute-done.8), channel_id=1, source_target_pairs={{0,2},{2,4},{4,6},{6,8},{8,10},{10,12},{12,14},{14,16},{16,18},{18... | collective-permute-start | bytes 393224 | tf_op jit(solution)/shard_map/ppermute | solution.py:35
  100.6 8.8 %copy-start.17 = (f32[16,1,2048]{2,1,0:T(1,128)}, f32[16,1,2048]{2,1,0:T(1,128)S(1)}, u32[]{:S(2)}) copy-start(f32[16,1,2048]{2,1,0:T(1,128)S(1)} %collective-permute-done.9) | copy-start | bytes 393220
  100.6 8.8 %collective-permute-start.10 = (f32[16,1,2048]{2,1,0:T(1,128)S(1)}, f32[16,1,2048]{2,1,0:T(1,128)}, u32[]{:S(2)}, u32[]{:S(2)}) collective-permute-start(f32[16,1,2048]{2,1,0:T(1,128)S(1)} %collective-permute-done.9), channel_id=1, source_target_pairs={{0,2},{2,4},{4,6},{6,8},{8,10},{10,12},{12,14},{14,16},{16,18},{18... | collective-permute-start | bytes 393224 | tf_op jit(solution)/shard_map/ppermute | solution.py:35
  109.4 1.8 %copy-start.19 = (s32[4]{0:T(128)S(1)}, s32[4]{0:T(128)}, u32[]{:S(2)}) copy-start(s32[4]{0:T(128)} %param.11) | copy-start | bytes 52
  109.4 48.6 %copy-start.2 = (f32[16,1,2048]{2,1,0:T(1,128)S(1)}, f32[16,1,2048]{2,1,0:T(1,128)}, u32[]{:S(2)}) copy-start(f32[16,1,2048]{2,1,0:T(1,128)} %param.13) | copy-start | bytes 393220
  109.4 8.9 %collective-permute-start.11 = (f32[16,1,2048]{2,1,0:T(1,128)}, f32[16,1,2048]{2,1,0:T(1,128)}, u32[]{:S(2)}, u32[]{:S(2)}) collective-permute-start(f32[16,1,2048]{2,1,0:T(1,128)} %collective-permute-done.10), channel_id=1, source_target_pairs={{0,2},{2,4},{4,6},{6,8},{8,10},{10,12},{12,14},{14,16},{16,18},{18... | collective-permute-start | bytes 393224 | tf_op jit(solution)/shard_map/ppermute | solution.py:35
  118.3 8.9 %collective-permute-start.12 = (f32[16,1,2048]{2,1,0:T(1,128)}, f32[16,1,2048]{2,1,0:T(1,128)}, u32[]{:S(2)}, u32[]{:S(2)}) collective-permute-start(f32[16,1,2048]{2,1,0:T(1,128)} %collective-permute-done.11), channel_id=1, source_target_pairs={{0,2},{2,4},{4,6},{6,8},{8,10},{10,12},{12,14},{14,16},{16,18},{18... | collective-permute-start | bytes 393224 | tf_op jit(solution)/shard_map/ppermute | solution.py:35
  127.2 10.0 %collective-permute-start.13 = (f32[16,1,2048]{2,1,0:T(1,128)}, f32[16,1,2048]{2,1,0:T(1,128)}, u32[]{:S(2)}, u32[]{:S(2)}) collective-permute-start(f32[16,1,2048]{2,1,0:T(1,128)} %collective-permute-done.12), channel_id=1, source_target_pairs={{0,2},{2,4},{4,6},{6,8},{8,10},{10,12},{12,14},{14,16},{16,18},{18... | collective-permute-start | bytes 393224 | tf_op jit(solution)/shard_map/ppermute | solution.py:35
  137.2 24.7 %copy-start.18 = (f32[16,1,2048]{2,1,0:T(1,128)S(1)}, f32[16,1,2048]{2,1,0:T(1,128)}, u32[]{:S(2)}) copy-start(f32[16,1,2048]{2,1,0:T(1,128)} %copy-done.17) | copy-start | bytes 393220
  137.2 24.7 %copy-start.16 = (f32[16,1,2048]{2,1,0:T(1,128)S(1)}, f32[16,1,2048]{2,1,0:T(1,128)}, u32[]{:S(2)}) copy-start(f32[16,1,2048]{2,1,0:T(1,128)} %copy-done.15) | copy-start | bytes 393220
  137.2 24.7 %copy-start.14 = (f32[16,1,2048]{2,1,0:T(1,128)S(1)}, f32[16,1,2048]{2,1,0:T(1,128)}, u32[]{:S(2)}) copy-start(f32[16,1,2048]{2,1,0:T(1,128)} %copy-done.13) | copy-start | bytes 393220
  137.2 24.8 %copy-start.12 = (f32[16,1,2048]{2,1,0:T(1,128)S(1)}, f32[16,1,2048]{2,1,0:T(1,128)}, u32[]{:S(2)}) copy-start(f32[16,1,2048]{2,1,0:T(1,128)} %copy-done.11) | copy-start | bytes 393220
  137.2 24.8 %copy-start.10 = (f32[16,1,2048]{2,1,0:T(1,128)S(1)}, f32[16,1,2048]{2,1,0:T(1,128)}, u32[]{:S(2)}) copy-start(f32[16,1,2048]{2,1,0:T(1,128)} %copy-done.9) | copy-start | bytes 393220
  137.2 24.8 %copy-start.8 = (f32[16,1,2048]{2,1,0:T(1,128)S(1)}, f32[16,1,2048]{2,1,0:T(1,128)}, u32[]{:S(2)}) copy-start(f32[16,1,2048]{2,1,0:T(1,128)} %copy-done.7) | copy-start | bytes 393220
  137.2 24.8 %copy-start.6 = (f32[16,1,2048]{2,1,0:T(1,128)S(1)}, f32[16,1,2048]{2,1,0:T(1,128)}, u32[]{:S(2)}) copy-start(f32[16,1,2048]{2,1,0:T(1,128)} %copy-done.5) | copy-start | bytes 393220
  137.2 24.9 %copy-start.4 = (f32[16,1,2048]{2,1,0:T(1,128)S(1)}, f32[16,1,2048]{2,1,0:T(1,128)}, u32[]{:S(2)}) copy-start(f32[16,1,2048]{2,1,0:T(1,128)} %copy-done.3) | copy-start | bytes 393220
  137.2 9.6 %collective-permute-start.14 = (f32[16,1,2048]{2,1,0:T(1,128)}, f32[16,1,2048]{2,1,0:T(1,128)S(1)}, u32[]{:S(2)}, u32[]{:S(2)}) collective-permute-start(f32[16,1,2048]{2,1,0:T(1,128)} %collective-permute-done.13), channel_id=1, source_target_pairs={{0,2},{2,4},{4,6},{6,8},{8,10},{10,12},{12,14},{14,16},{16,18},{18... | collective-permute-start | bytes 393224 | tf_op jit(solution)/shard_map/ppermute | solution.py:35
  (4 other events, 2.6 us)
Sparse Core Ops, SparseCore 0:
  111.4 20.0 all-reduce.2
